TPU v7x, 256 devices: a whole 4x4x8 slice. The times are simulated.
256 devices in a mesh: row: 16 (over x, z_hi, core), col: 16 (over z_lo, y).
Axes of the slice: x: 4, y: 4, z: 8 (z_hi: 2, z_lo: 4; z = z_hi * 4 + z_lo), core: 2. Of those that a mesh axis runs over, the one named last changes fastest.
Arguments:
- ancestor_inverse: bfloat16 [24576, 24576], P('row', 'col'), may hold values from -0.0390625 to 0.0390625
- panels: bfloat16 [24576, 3, 512], P(('row', 'col')), may hold values from -1.1953125 to 1.1953125
- diag_inverse: float32 [3, 512, 512], replicated, may hold values from -6 to 6
- tile_mask: int32 [3, 192], replicated, may hold values 0 or 1
Outputs:
- off_diagonal: float32 [24576, 3, 512], P(('row', 'col'))
- diagonal: float32 [3, 512, 512], replicated
All inputs are finite; a program needn't handle non-finite values.
Results may differ from a plain program's by a relative error of at most 0.0003.
Values may be sent and summed in bfloat16 or wider, within the bound.
No kernel may reach another device: no remote copies, remote signals or barrier semaphores. Data moves between devices by JAX's collectives and lax.ppermute only.
A program may use at most 192 MiB of HBM per device.

v0:
```python
import jax
import jax.numpy as jnp
from jax import lax
from jax.sharding import Mesh
from jax.sharding import PartitionSpec as P

TILE = 128
COL = ("col_0", "col_1")
ROW_COL = ("row", "col_0", "col_1")


def in_order(tiles, dim):
    tiles = jnp.moveaxis(tiles, 0, dim)
    dims = tiles.shape
    return tiles.reshape(*dims[:dim], dims[dim] * dims[dim + 1], *dims[dim + 2 :])


def stacked_from(shard, axes, sequence):
    tiles = shard
    for k in sequence:
        tiles = lax.all_gather(tiles, axes[k])
    done = sequence[::-1]
    back = [done.index(k) for k in range(len(axes))]
    tiles = tiles.transpose(*back, *range(len(axes), tiles.ndim))
    return tiles.reshape(-1, *shard.shape)


def gathered_by_axis(shard, axes, sequence, dim):
    return in_order(stacked_from(shard, axes, sequence), dim)


def filled_up(lines, devices):
    spare = -lines.shape[0] % devices
    if not spare:
        return lines
    return jnp.concatenate([lines, jnp.zeros((spare, *lines.shape[1:]), lines.dtype)])


def from_root(shard, axis, root):
    lines = jnp.where(lax.axis_index(axis) == root, shard, jnp.zeros_like(shard)).reshape(
        -1, *shard.shape[1:][-1:]
    )
    padded = filled_up(lines, lax.axis_size(axis))
    own = lax.psum_scatter(padded, axis, scatter_dimension=0, tiled=True)
    return lax.all_gather(own, axis, axis=0, tiled=True)[: len(lines)].reshape(shard.shape)


def make_term(ancestor_inverse, right_side):
    return jnp.dot(ancestor_inverse, right_side, preferred_element_type=jnp.float32)


def body(ancestor_inverse, panels, diag_inverse, tile_mask):
    row_count = lax.axis_size("row")
    col_count = lax.axis_size(COL)
    col_index = lax.axis_index(COL)
    row_index = lax.axis_index("row")
    kept_rows = panels.shape[0]
    panel_count = panels.shape[1]
    width_cols = panels.shape[2]
    matrix_order = kept_rows * row_count * col_count
    block_rows = matrix_order // col_count
    full_mask = jnp.repeat(tile_mask, TILE, axis=1).T.astype(jnp.bfloat16)
    gathered = gathered_by_axis(panels, COL, (0, 1), 0)
    col_group = col_count // row_count
    root_row = col_index // col_group
    partner = from_root(gathered, "row", root_row)
    col_mask = lax.dynamic_slice_in_dim(full_mask, col_index * block_rows, block_rows, 0)
    masked_col = partner * col_mask[:, :, None]
    flattened = masked_col.reshape(block_rows, panel_count * width_cols)
    summed = lax.psum_scatter(
        make_term(ancestor_inverse, flattened), COL, scatter_dimension=0, tiled=True
    )
    off_diagonal = -summed.reshape(kept_rows, panel_count, width_cols)
    span_start = (row_index * col_count + col_index) * kept_rows
    own_mask = lax.dynamic_slice_in_dim(full_mask, span_start, kept_rows, 0)
    masked_own = (panels * own_mask[:, :, None]).astype(jnp.float32)
    schur_part = jnp.einsum(
        "mpa,mpb->pab", masked_own, off_diagonal, precision=lax.Precision.HIGHEST
    )
    schur_total = lax.psum(schur_part, ROW_COL)
    diagonal = diag_inverse - schur_total
    return (off_diagonal, diagonal)


def solution(mesh):
    finer = Mesh(mesh.devices.reshape(mesh.shape["row"], 4, 4), ("row", "col_0", "col_1"))
    placed = (P("row", COL), P(ROW_COL, None, None), P(), P())
    return jax.shard_map(
        body, mesh=finer, in_specs=placed, out_specs=(P(ROW_COL, None, None), P()), check_vma=False
    )
```

profile of v0, /device:TPU:1, one launch (start us, length us, event | category | flops | bytes accessed | tf_op | source)
XLA Modules:
  0.0 741.3 jit_solution(1819610652847261270)
XLA Ops:
  7.2 0.0 all-gather.8.cloned.1.call-start
  7.2 0.7 all-gather.8.cloned.1.call-update
  7.9 0.0 all-gather.10.cloned.1.call-start
  7.9 41.0 %all-gather.8.cloned.1.call-done = bf16[384,3,512]{2,0,1:T(8,128)(2,1)} async-done(((bf16[96,3,512]{2,0,1:T(8,128)(2,1)}), bf16[384,3,512]{2,0,1:T(8,128)(2,1)}) %all-gather.8.cloned.1.call-update) | async-done | bytes 1179664 | tf_op jit(solution)/shard_map/all_gather | solution.py:21
  49.0 0.0 all-gather.10.cloned.1.call-update
  49.0 0.0 reduce-scatter.5.cloned.1.call-start
  49.1 56.3 %all-gather.10.cloned.1.call-done = bf16[16,96,3,512]{3,1,0,2:T(8,128)(2,1)} async-done(((bf16[4,96,3,512]{3,1,0,2:T(8,128)(2,1)}), bf16[16,96,3,512]{3,1,0,2:T(8,128)(2,1)}) %all-gather.10.cloned.1.call-update) | async-done | bytes 4718608 | tf_op jit(solution)/shard_map/all_gather | solution.py:21
  105.3 0.3 broadcast_select_fusion
  105.6 6.7 copy.22
  112.4 12.3 %select_n.27 = bf16[4608,512]{1,0:T(8,128)(2,1)} reshape(bf16[4,4,96,3,512]{4,3,2,1,0:T(4,128)(2,1)} %copy.22) | data formatting | bytes 9437184 | tf_op jit(solution)/shard_map/jit(_where)/select_n | solution.py:40
  124.7 0.0 all-gather.6.cloned.1.call-start
  124.8 108.3 %reduce-scatter.5.cloned.1.call-done = bf16[288,512]{1,0:T(8,128)(2,1)} async-done(((bf16[4608,512]{1,0:T(8,128)(2,1)}), bf16[288,512]{1,0:T(8,128)(2,1)}) %reduce-scatter.5.cloned.1.call-update) | async-done | bytes 294928 | tf_op jit(solution)/shard_map/reduce_scatter | solution.py:44
  233.1 0.0 all-gather.6.cloned.1.call-update
  233.1 0.0 reduce-scatter.7.cloned.1.call-start
  233.2 0.1 broadcast_bitcast_fusion
  233.3 0.1 copy.32
  233.5 81.1 %all-gather.6.cloned.1.call-done = bf16[4608,512]{1,0:T(8,128)(2,1)} async-done(((bf16[288,512]{1,0:T(8,128)(2,1)}), bf16[4608,512]{1,0:T(8,128)(2,1)}) %all-gather.6.cloned.1.call-update) | async-done | bytes 4718608 | tf_op jit(solution)/shard_map/all_gather | solution.py:45
  314.6 8.3 %reshape.21 = bf16[1536,1536]{1,0:T(8,128)(2,1)} reshape(bf16[4608,512]{1,0:T(8,128)(2,1)} %all-gather.6.cloned.1.call-done) | data formatting | bytes 9437184 | tf_op jit(solution)/shard_map/reshape | solution.py:45
  322.9 6.6 copy.23
  329.5 2.6 bitcast_multiply_fusion
  332.2 11.9 %convolution_bitcast_fusion = f32[1536,1536]{0,1:T(8,128)} fusion(bf16[1536,1536]{0,1:T(8,128)(2,1)S(1)} %bitcast_multiply_fusion, bf16[1536,1536]{1,0:T(8,128)(2,1)} %param.4), kind=kOutput, calls=%fused_computation | convolution fusion | flops 7247757312 | bytes 18874368 | tf_op jit(solution)/shard_map/dot_general | solution.py:49
  344.1 9.6 %copy.28 = f32[1536,1536]{1,0:T(8,128)} copy(f32[1536,1536]{0,1:T(8,128)} %convolution_bitcast_fusion) | data formatting | bytes 18874368
  353.8 0.0 reduce-scatter.7.cloned.1.call-update
  353.8 0.2 all-reduce.2.cloned.1.call-start
  354.0 0.1 dynamic-slice_bitcast_fusion.1
  354.1 108.2 %reduce-scatter.7.cloned.1.call-done = f32[96,1536]{1,0:T(8,128)} async-done(((f32[1536,1536]{1,0:T(8,128)}), f32[96,1536]{1,0:T(8,128)}) %reduce-scatter.7.cloned.1.call-update) | async-done | bytes 589840
  462.3 1.3 copy.29
  463.7 0.1 neg.6
  463.7 3.3 fusion
  467.0 1.1 copy.25
  468.1 261.1 %all-reduce.2.cloned.1.call-done = f32[3,512,512]{2,1,0:T(8,128)} async-done(((f32[3,512,512]{2,1,0:T(8,128)}), f32[3,512,512]{2,1,0:T(8,128)}) %all-reduce.2.cloned.1.call-update) | async-done | bytes 3145744 | tf_op jit(solution)/shard_map/psum | solution.py:80
  729.2 5.3 sub.5
  (8 shorter events, 0.1 us)
Async XLA Ops:
  7.2 41.8 %all-gather.8.cloned.1.call-start = ((), (), s32[]{:S(2)}) async-start(), calls=%async_computation.5 | async-start | bytes 1474560 | tf_op jit(solution)/shard_map/all_gather | solution.py:21
  7.9 97.4 %all-gather.10.cloned.1.call-start = ((), (), s32[]{:S(2)}) async-start(), calls=%async_computation.6 | async-start | bytes 5898240 | tf_op jit(solution)/shard_map/all_gather | solution.py:21
  49.0 184.1 %reduce-scatter.5.cloned.1.call-start = ((), (), s32[]{:S(2)}) async-start(), calls=%async_computation.2 | async-start | bytes 5013504 | tf_op jit(solution)/shard_map/reduce_scatter | solution.py:44
  124.7 108.4 %copy-start.1 = (s32[3,192]{1,0:T(4,128)S(1)}, s32[3,192]{1,0:T(4,128)}, u32[]{:S(2)}) copy-start(s32[3,192]{1,0:T(4,128)} %param.7) | copy-start | bytes 6916
  124.7 189.8 %all-gather.6.cloned.1.call-start = ((), (), s32[]{:S(2)}) async-start(), calls=%async_computation.3 | async-start | bytes 5013504 | tf_op jit(solution)/shard_map/all_gather | solution.py:45
  233.1 229.2 %reduce-scatter.7.cloned.1.call-start = ((), (), s32[]{:S(2)}) async-start(), calls=%async_computation.7 | async-start | bytes 10027008
  353.8 110.0 %copy-start = (bf16[96,3,512]{2,0,1:T(8,128)(2,1)S(1)}, bf16[96,3,512]{2,0,1:T(8,128)(2,1)}, u32[]{:S(2)}) copy-start(bf16[96,3,512]{2,0,1:T(8,128)(2,1)} %param.5) | copy-start | bytes 884740
  353.8 375.4 %all-reduce.2.cloned.1.call-start = ((), (), s32[]{:S(2)}) async-start(), calls=%async_computation.4 | async-start | bytes 6291456 | tf_op jit(solution)/shard_map/psum | solution.py:80
Sparse Core Ops, SparseCore 0:
  9.8 39.1 all-gather.7
  50.8 54.4 all-gather.9
  124.9 108.1 reduce-scatter.4
  236.0 78.5 all-gather.5
  353.9 108.3 reduce-scatter.6
  469.1 260.1 all-reduce.1
where the time goes:
time: 743 us; the launch traced here: 741 us
  waiting for transfers between devices  657 us (88%)
  local copies, waits for them, and re-layouts  46.4 us (6%)
  matrix products  15.2 us (2%)
  between operations  14.2 us (2%)
  other arithmetic  8.27 us (1%)
    psum x1, waiting for transfers between devices, body(): schur_total = lax.psum(schur_part, ROW_COL)  261 us
    unnamed x7, waiting for transfers between devices  109 us
    reduce_scatter x1, waiting for transfers between devices, from_root(): own = lax.psum_scatter(padded, axis, scatter_dimension=0, tiled=True)  108 us
    all_gather x2, waiting for transfers between devices, stacked_from(): tiles = lax.all_gather(tiles, axes[k])  97.3 us
    all_gather x1, waiting for transfers between devices, from_root(): lax.all_gather(own, axis, axis=0, tiled=True)[:len(lines)]  81.1 us
    select_n x2, local copies, waits for them, and re-layouts, from_root(): jnp.where(lax.axis_index(axis) == root, shard, jnp.zeros_like(shard))  19.1 us
    reshape x2, local copies, waits for them, and re-layouts, from_root(): lax.all_gather(own, axis, axis=0, tiled=True)[:len(lines)]  14.9 us
  transfers between devices with their start and end apart: 6, of which 6 were waited for; matrix products, arithmetic and copies ran while one was open for 0% of the time, Pallas kernels for 0%

commit v1 on v0

v1 whole, which is shorter than its diff:
```python
import jax
import jax.numpy as jnp
from jax import lax
from jax.sharding import PartitionSpec as P

TILE = 128
ALL = ("row", "col")


def body(ancestor_inverse, panels, diag_inverse, tile_mask):
    rows, cols = lax.axis_size("row"), lax.axis_size("col")
    row_index, col_index = lax.axis_index("row"), lax.axis_index("col")
    kept, count, width = panels.shape
    start = (row_index * cols + col_index) * kept
    tile_of = (start + jnp.arange(kept)) // TILE
    own_mask = jnp.take(tile_mask, tile_of, axis=1).astype(jnp.bfloat16)
    masked = jnp.swapaxes(panels, 0, 1) * own_mask[:, :, None]
    flip = [(i * cols + j, j * cols + i) for i in range(rows) for j in range(cols)]
    turned = lax.ppermute(masked, ALL, flip)
    blocks = []
    for p in range(count):
        gathered = lax.all_gather(turned[p], "row", axis=0, tiled=True)
        partial = jnp.dot(ancestor_inverse, gathered, preferred_element_type=jnp.float32)
        summed = lax.psum_scatter(partial, "col", scatter_dimension=0, tiled=True)
        blocks.append(-summed)
    off_diagonal = jnp.stack(blocks)
    schur = jnp.einsum(
        "pma,pmb->pab",
        masked.astype(jnp.float32),
        off_diagonal,
        precision=lax.Precision.HIGHEST,
    )
    lines = schur.reshape(count * width, width)
    share = lax.psum_scatter(lines, "col", scatter_dimension=0, tiled=True)
    share = lax.psum(share, "row")
    total = lax.all_gather(share, "col", axis=0, tiled=True)
    return jnp.swapaxes(off_diagonal, 0, 1), diag_inverse - total.reshape(schur.shape)


def solution(mesh):
    placed = (P("row", "col"), P(ALL, None, None), P(), P())
    return jax.shard_map(
        body, mesh=mesh, in_specs=placed, out_specs=(P(ALL, None, None), P()), check_vma=False
    )
```

time: 743 us -> 856 us (1.15)
  waiting for transfers between devices: 657 us -> 790 us
  local copies, waits for them, and re-layouts: 46.4 us -> 10 us
    reduce_scatter x1 -> x4, waiting for transfers between devices: 108 us -> 338 us  [the longest x3 250 us: body(): summed = lax.psum_scatter(partial, 'col', scatter_dimension=0, tiled=True)]
    unnamed x7 -> x9, waiting for transfers between devices: 109 us -> 1.49 us
    all_gather x3 -> x4, waiting for transfers between devices: 178 us -> 268 us  [the longest x3 192 us: body(): gathered = lax.all_gather(turned[p], 'row', axis=0, tiled=True)]
    psum x1, waiting for transfers between devices: 261 us -> 178 us  [body(): share = lax.psum(share, 'row')]
    select_n x2 -> x0, local copies, waits for them, and re-layouts: 19.1 us -> none  [from_root(): jnp.where(lax.axis_index(axis) == root, shard, jnp.zeros_like(shard))]
    reshape x2 -> x0, local copies, waits for them, and re-layouts: 14.9 us -> none  [from_root(): lax.all_gather(own, axis, axis=0, tiled=True)[:len(lines)]]
    dot_general x2 -> x4, matrix products: 15.2 us -> 18.1 us  [the longest x3 15.1 us: body(): jnp.dot(ancestor_inverse, gathered, preferred_element_type=jnp.float32)]
  transfers between devices with their start and end apart: 6 -> 10, of which waited for: 6 -> 10; matrix products, arithmetic and copies ran while one was open for 0% -> 3% of each run, Pallas kernels for 0% -> 0%
where the time goes in v1:
time: 856 us; the launch traced here: 847 us
  waiting for transfers between devices  790 us (92%)
  matrix products  18.1 us (2%)
  between operations  13.9 us (2%)
  other arithmetic  10.1 us (1%)
  local copies, waits for them, and re-layouts  10 us (1%)
    reduce_scatter x3, waiting for transfers between devices, body(): summed = lax.psum_scatter(partial, 'col', scatter_dimension=0, tiled=True)  250 us
    all_gather x3, waiting for transfers between devices, body(): gathered = lax.all_gather(turned[p], 'row', axis=0, tiled=True)  192 us
    psum x1, waiting for transfers between devices, body(): share = lax.psum(share, 'row')  178 us
    reduce_scatter x1, waiting for transfers between devices, body(): share = lax.psum_scatter(lines, 'col', scatter_dimension=0, tiled=True)  87.6 us
    all_gather x1, waiting for transfers between devices, body(): total = lax.all_gather(share, 'col', axis=0, tiled=True)  76 us
  transfers between devices with their start and end apart: 10, of which 10 were waited for; matrix products, arithmetic and copies ran while one was open for 3% of the time, Pallas kernels for 0%

profile of v1, /device:TPU:1, one launch (start us, length us, event | category | flops | bytes accessed | tf_op | source)
XLA Modules:
  0.0 846.9 jit_solution(13379166648206793179)
XLA Ops:
  7.3 0.8 copy.10
  8.1 0.6 gather_fusion
  8.7 0.1 fusion.5
  8.8 0.1 copy.11
  8.9 1.1 bitcast_multiply_fusion
  10.0 4.6 collective-permute-start
  14.6 4.4 collective-permute-done
  18.9 0.7 fusion.8
  19.7 0.7 all-gather.12.cloned.1.call-update
  20.5 0.7 all-gather.10.cloned.1.call-update
  21.2 90.2 %all-gather.14.cloned.1.call-done = bf16[1,1536,512]{2,1,0:T(8,128)(2,1)} async-done(((bf16[1,96,512]{2,1,0:T(8,128)(2,1)}), bf16[1,1536,512]{2,1,0:T(8,128)(2,1)}) %all-gather.14.cloned.1.call-update) | async-done | bytes 1572880 | tf_op jit(solution)/shard_map/all_gather | solution.py:22
  111.4 5.0 convolution_bitcast_fusion
  116.4 2.4 copy.19
  118.9 50.4 %all-gather.12.cloned.1.call-done = bf16[1,1536,512]{2,1,0:T(8,128)(2,1)} async-done(((bf16[1,96,512]{2,1,0:T(8,128)(2,1)}), bf16[1,1536,512]{2,1,0:T(8,128)(2,1)}) %all-gather.12.cloned.1.call-update) | async-done | bytes 1572880 | tf_op jit(solution)/shard_map/all_gather | solution.py:22
  169.3 5.0 convolution_bitcast_fusion.1
  174.3 2.4 copy.17
  176.7 51.0 %all-gather.10.cloned.1.call-done = bf16[1,1536,512]{2,1,0:T(8,128)(2,1)} async-done(((bf16[1,96,512]{2,1,0:T(8,128)(2,1)}), bf16[1,1536,512]{2,1,0:T(8,128)(2,1)}) %all-gather.10.cloned.1.call-update) | async-done | bytes 1572880 | tf_op jit(solution)/shard_map/all_gather | solution.py:22
  227.7 5.0 convolution_bitcast_fusion.2
  232.8 2.4 copy.15
  235.2 72.0 %reduce-scatter.17.cloned.1.call-done = f32[96,512]{1,0:T(8,128)} async-done(((f32[1536,512]{1,0:T(8,128)}), f32[96,512]{1,0:T(8,128)}) %reduce-scatter.17.cloned.1.call-update) | async-done | bytes 196624 | tf_op jit(solution)/shard_map/reduce_scatter | solution.py:24
  307.3 0.9 negate_bitcast_fusion
  308.2 89.1 %reduce-scatter.15.cloned.1.call-done = f32[96,512]{1,0:T(8,128)} async-done(((f32[1536,512]{1,0:T(8,128)}), f32[96,512]{1,0:T(8,128)}) %reduce-scatter.15.cloned.1.call-update) | async-done | bytes 196624 | tf_op jit(solution)/shard_map/reduce_scatter | solution.py:24
  397.3 0.9 negate_bitcast_fusion.1
  398.3 89.0 %reduce-scatter.13.cloned.1.call-done = f32[96,512]{1,0:T(8,128)} async-done(((f32[1536,512]{1,0:T(8,128)}), f32[96,512]{1,0:T(8,128)}) %reduce-scatter.13.cloned.1.call-update) | async-done | bytes 196624 | tf_op jit(solution)/shard_map/reduce_scatter | solution.py:24
  487.3 0.9 negate_bitcast_fusion.2
  488.2 0.7 copy-done.1
  488.9 3.1 fusion.3
  492.1 87.6 %reduce-scatter.11.cloned.1.call-done = f32[96,512]{1,0:T(8,128)} async-done(((f32[1536,512]{1,0:T(8,128)}), f32[96,512]{1,0:T(8,128)}) %reduce-scatter.11.cloned.1.call-update) | async-done | bytes 196624 | tf_op jit(solution)/shard_map/reduce_scatter | solution.py:34
  579.8 178.5 %all-reduce.2.cloned.1.call-done = f32[96,512]{1,0:T(8,128)} async-done(((f32[96,512]{1,0:T(8,128)}), f32[96,512]{1,0:T(8,128)}) %all-reduce.2.cloned.1.call-update) | async-done | bytes 196624 | tf_op jit(solution)/shard_map/psum | solution.py:35
  758.3 1.8 fusion.4
  760.1 76.0 %all-gather.8.cloned.1.call-done = f32[1536,512]{1,0:T(8,128)} async-done(((f32[96,512]{1,0:T(8,128)}), f32[1536,512]{1,0:T(8,128)}) %all-gather.8.cloned.1.call-update) | async-done | bytes 3145744 | tf_op jit(solution)/shard_map/all_gather | solution.py:36
  836.0 4.3 sub.13
  (22 shorter events, 0.5 us)
Async XLA Ops:
  7.2 104.2 %all-gather.14.cloned.1.call-start = ((), (), s32[]{:S(2)}) async-start(), calls=%async_computation.9 | async-start | bytes 1671168 | tf_op jit(solution)/shard_map/all_gather | solution.py:22
  10.0 9.0 %collective-permute-start = (bf16[3,96,512]{2,1,0:T(8,128)(2,1)S(1)}, bf16[3,96,512]{2,1,0:T(8,128)(2,1)S(1)}, u32[]{:S(2)}, u32[]{:S(2)}) collective-permute-start(bf16[3,96,512]{2,1,0:T(8,128)(2,1)S(1)} %bitcast_multiply_fusion), channel_id=1, source_target_pairs={{0,0},{1,16},{2,32},{3,48},{4,64},{5,80},{6,96},{7,112},{8,128},{9... | collective-permute-start | bytes 884744 | tf_op jit(solution)/shard_map/ppermute | solution.py:19
  19.7 149.6 %all-gather.12.cloned.1.call-start = ((), (), s32[]{:S(2)}) async-start(), calls=%async_computation.8 | async-start | bytes 1671168 | tf_op jit(solution)/shard_map/all_gather | solution.py:22
  20.4 207.3 %all-gather.10.cloned.1.call-start = ((), (), s32[]{:S(2)}) async-start(), calls=%async_computation.7 | async-start | bytes 1671168 | tf_op jit(solution)/shard_map/all_gather | solution.py:22
  21.2 286.1 %reduce-scatter.17.cloned.1.call-start = ((), (), s32[]{:S(2)}) async-start(), calls=%async_computation.12 | async-start | bytes 3342336 | tf_op jit(solution)/shard_map/reduce_scatter | solution.py:24
  118.8 278.5 %reduce-scatter.15.cloned.1.call-start = ((), (), s32[]{:S(2)}) async-start(), calls=%async_computation.11 | async-start | bytes 3342336 | tf_op jit(solution)/shard_map/reduce_scatter | solution.py:24
  176.7 310.6 %reduce-scatter.13.cloned.1.call-start = ((), (), s32[]{:S(2)}) async-start(), calls=%async_computation.10 | async-start | bytes 3342336 | tf_op jit(solution)/shard_map/reduce_scatter | solution.py:24
  235.2 344.5 %reduce-scatter.11.cloned.1.call-start = ((), (), s32[]{:S(2)}) async-start(), calls=%async_computation.4 | async-start | bytes 3342336 | tf_op jit(solution)/shard_map/reduce_scatter | solution.py:34
  488.2 0.7 copy-start.1
  492.0 344.0 %copy-start = (f32[3,512,512]{2,1,0:T(8,128)S(1)}, f32[3,512,512]{2,1,0:T(8,128)}, u32[]{:S(2)}) copy-start(f32[3,512,512]{2,1,0:T(8,128)} %param.6) | copy-start | bytes 9437188
  492.0 266.2 %all-reduce.2.cloned.1.call-start = ((), (), s32[]{:S(2)}) async-start(), calls=%async_computation.5 | async-start | bytes 393216 | tf_op jit(solution)/shard_map/psum | solution.py:35
  579.7 256.3 %all-gather.8.cloned.1.call-start = ((), (), s32[]{:S(2)}) async-start(), calls=%async_computation.6 | async-start | bytes 3342336 | tf_op jit(solution)/shard_map/all_gather | solution.py:36
Sparse Core Ops, SparseCore 0:
  19.8 91.5 all-gather.13
  114.1 55.1 all-gather.11
  172.5 55.1 all-gather.9
  230.7 76.4 reduce-scatter.16
  309.7 87.5 reduce-scatter.14
  399.7 87.5 reduce-scatter.12
  492.2 87.5 reduce-scatter.10
  582.3 175.8 all-reduce.1
  760.2 75.7 all-gather.7
